TPU v7x, 32 devices: a whole 2x2x4 slice. The times are simulated.
32 devices in a mesh: fsdp: 8 (over y, x, core), dp: 4 (over z).
Axes of the slice: x: 2, y: 2, z: 4, core: 2. Of those that a mesh axis runs over, the one named last changes fastest.
Arguments:
- hidden: bfloat16 [8192, 14336], P(('fsdp', 'dp')), may hold values from -6 to 6
- cotangent: bfloat16 [8192, 4096], P(('fsdp', 'dp')), may hold values from -6 to 6
- tiles: bfloat16 [64, 128, 128], P('fsdp'), may hold values from -0.25 to 0.25
- tile_rows: int32 [64], P('fsdp'), may hold values from 0 to 111, as said below
- tile_cols: int32 [64], P('fsdp'), may hold values from 0 to 31, as said below
- counts: int32 [8], P('fsdp'), may hold values from 1 to 8, as said below
Outputs:
- layer_out: bfloat16 [8192, 4096], P(('fsdp', 'dp'))
- hidden_grad: bfloat16 [8192, 14336], P(('fsdp', 'dp'))
- weight_grad: float32 [64, 128, 128], P('fsdp')
Inputs may be any that keep to these rules, and one draw needn't show every extreme that they name: `tile_rows`: every slot (live or not) names a different block; the row block is below 112. `tile_cols`: the column block is below 32. `counts`: some owner has all 8 slots live in every draw.
All inputs are finite; a program needn't handle non-finite values.
Results may differ from a plain program's by a relative error of at most 0.0085.
Values may be sent and summed in bfloat16 or wider, within the bound.
A program may use at most 192 MiB of HBM per device.

v0:
```python
import math

import jax
import jax.numpy as jnp
from jax import lax
from jax.sharding import PartitionSpec as P


def one_hot_of(ids, width):
    return (ids[:, None] == jnp.arange(width, dtype=jnp.int32)[None, :]).astype(jnp.bfloat16)


def select_blocks(blocks, ids):
    table = one_hot_of(ids, blocks.shape[1])
    chosen = jnp.einsum("tbe,kb->tke", blocks, table, preferred_element_type=jnp.float32)
    return chosen.astype(jnp.bfloat16)


def place_blocks(partial_value, ids, width):
    table = one_hot_of(ids, width).astype(jnp.float32)
    return jnp.einsum("tke,kb->tbe", partial_value, table)


def shards(hidden, cotangent, tiles, tile_rows, tile_cols, counts):
    tokens = hidden.shape[0]
    slots_own = tiles.shape[0]
    edge_len = tiles.shape[1]
    blocks_ff = hidden.shape[1] // edge_len
    blocks_model = cotangent.shape[1] // edge_len
    live_slots = jnp.arange(slots_own) < counts[0]
    masked = jnp.where(live_slots[:, None, None], tiles, jnp.zeros_like(tiles))
    all_rows, all_cols = (
        lax.all_gather(tile_rows, "fsdp", axis=0, tiled=True),
        lax.all_gather(tile_cols, "fsdp", axis=0, tiled=True),
    )
    hidden_blocks = hidden.reshape(tokens, blocks_ff, edge_len)
    upstream_blocks = cotangent.reshape(tokens, blocks_model, edge_len)
    gathered = lax.all_gather(masked, "fsdp", axis=0, tiled=True)
    row_ids = all_rows
    col_ids = all_cols
    picked = select_blocks(hidden_blocks, row_ids)
    partial_value = jnp.einsum("tkf,kfd->tkd", picked, gathered, preferred_element_type=jnp.float32)
    layer_acc = place_blocks(partial_value, col_ids, blocks_model)
    row_ids = all_rows
    col_ids = all_cols
    upstream = select_blocks(upstream_blocks, col_ids)
    partial_value = jnp.einsum(
        "tkd,kfd->tkf", upstream, gathered, preferred_element_type=jnp.float32
    )
    grad_acc = place_blocks(partial_value, row_ids, blocks_ff)
    row_ids = all_rows
    col_ids = all_cols
    picked = select_blocks(hidden_blocks, row_ids)
    upstream = select_blocks(upstream_blocks, col_ids)
    owned = lax.psum_scatter(
        jnp.einsum("tkf,tkd->kfd", picked, upstream, preferred_element_type=jnp.float32),
        "fsdp",
        scatter_dimension=0,
        tiled=True,
    )
    summed = lax.psum(owned, "dp")
    raw_grad = jnp.where(live_slots[:, None, None], summed, jnp.zeros_like(summed))
    local_squares = jnp.sum(raw_grad * raw_grad)
    local_entries = counts[0].astype(jnp.float32) * edge_len * edge_len
    squares, entries = lax.psum((local_squares, local_entries), "fsdp")
    spread = jnp.sqrt(squares / entries)
    root_tokens = math.sqrt(tokens * lax.axis_size("fsdp") * lax.axis_size("dp"))
    factor = jnp.minimum(1.0, 0.5 * root_tokens / spread) / root_tokens
    layer_out = layer_acc.reshape(tokens, blocks_model * edge_len).astype(jnp.bfloat16)
    hidden_grad = grad_acc.reshape(tokens, blocks_ff * edge_len).astype(jnp.bfloat16)
    return (layer_out, hidden_grad, raw_grad * factor)


def solution(mesh):
    placed = (
        P(("fsdp", "dp"), None),
        P(("fsdp", "dp"), None),
        P("fsdp", None, None),
        P("fsdp"),
        P("fsdp"),
        P("fsdp"),
    )
    return jax.shard_map(
        shards,
        mesh=mesh,
        in_specs=placed,
        out_specs=(P(("fsdp", "dp"), None), P(("fsdp", "dp"), None), P("fsdp", None, None)),
        check_vma=False,
    )
```

profile of v0, /device:TPU:0, one launch (start us, length us, event | category | flops | bytes accessed | tf_op | source)
XLA Modules:
  0.0 171.5 jit_solution(11835242717945344327)
XLA Ops:
  7.9 1.7 %broadcast_select_fusion = bf16[8,128,128]{2,1,0:T(8,128)(2,1)} fusion(bf16[8,128,128]{2,1,0:T(8,128)(2,1)} %param.8, pred[8]{0:T(512)(128)(4,1)S(1)} %iota_compare_fusion.2), kind=kLoop, calls=%fused_computation.16 | loop fusion | flops 131072 | bytes 524296 | tf_op jit(solution)/shard_map/jit(_where)/select_n | solution.py:31
  9.7 7.8 %copy.16 = bf16[32,8,112,128]{3,2,1,0:T(8,128)(2,1)} copy(bf16[32,8,112,128]{3,1,2,0:T(8,128)(2,1)} %bitcast.50) | data formatting | bytes 14680064
  17.6 0.6 dynamic-slice
  18.7 0.2 dynamic-update-slice
  19.2 9.7 %all-reduce.2 = (s32[64]{0:T(128)S(1)}, s32[64]{0:T(128)S(1)}) all-reduce(s32[64]{0:T(128)S(1)} %dynamic-update-slice.1, s32[64]{0:T(128)S(1)} %dynamic-update-slice), channel_id=1, replica_groups=mesh['fsdp'=8,'dp'=4] {'fsdp'}, use_global_device_ids=true, to_apply=%add.1 | all-reduce | flops 128 | bytes 1024
  28.9 6.4 %convert_bitcast_fusion.1 = bf16[256,64,128]{2,1,0:T(8,128)(2,1)} fusion(bf16[256,112,128]{2,1,0:T(8,128)(2,1)} %bitcast.46, s32[64]{0:T(128)S(1)} %get-tuple-element.3), kind=kOutput, calls=%fused_computation.7 | convolution fusion | flops 471866368 | bytes 11534592 | tf_op jit(solution)/shard_map/tbe,kb->tke/dot_general | solution.py:15
  35.3 7.1 %copy.11 = bf16[256,64,128]{0,2,1:T(8,128)(2,1)} copy(bf16[256,64,128]{2,1,0:T(8,128)(2,1)} %convert_bitcast_fusion.1) | data formatting | bytes 8388608 | tf_op jit(solution)/shard_map/convert_element_type | solution.py:16
  42.3 0.5 copy.18
  42.8 1.3 convert_bitcast_fusion
  44.1 2.0 %copy-done.1 = bf16[256,64,128]{2,1,0:T(8,128)(2,1)} copy-done((bf16[256,64,128]{2,1,0:T(8,128)(2,1)}, bf16[256,64,128]{2,1,0:T(8,128)(2,1)S(1)}, u32[]{:S(2)}) %copy-start.1) | copy-done | bytes 4194328
  46.1 7.2 %fusion.9 = f32[64,128,128]{2,1,0:T(8,128)} fusion(bf16[256,64,128]{0,2,1:T(8,128)(2,1)S(1)} %copy-done, bf16[256,64,128]{2,1,0:T(8,128)(2,1)S(1)} %convert_bitcast_fusion), kind=kOutput, calls=%fused_computation.10 | convolution fusion | flops 536870912 | bytes 12582912 | tf_op jit(solution)/shard_map/tkf,tkd->kfd/dot_general | solution.py:56
  53.6 9.4 %fusion.7 = bf16[64,128,256]{2,1,0:T(8,128)(2,1)} fusion(bf16[64,128,128]{2,1,0:T(8,128)(2,1)} %all-gather.2.cloned.1.call-done, bf16[256,64,128]{2,1,0:T(8,128)(2,1)} %copy-done.1), kind=kOutput, calls=%fused_computation.8 | convolution fusion | flops 536870912 | bytes 10485760 | tf_op jit(solution)/shard_map/tkd,kfd->tkf/dot_general | solution.py:47
  63.0 6.6 %copy.15 = bf16[64,128,256]{1,0,2:T(8,128)(2,1)} copy(bf16[64,128,256]{2,1,0:T(8,128)(2,1)} %fusion.7) | data formatting | bytes 8388608 | tf_op jit(solution)/shard_map/tkd,kfd->tkf/dot_general | solution.py:47
  69.7 7.6 %fusion.4 = bf16[112,256,128]{2,0,1:T(8,128)(2,1)} fusion(bf16[64,128,256]{1,0,2:T(8,128)(2,1)} %copy.15, s32[64]{0:T(128)S(1)} %get-tuple-element.3), kind=kOutput, calls=%fused_computation.5 | convolution fusion | flops 469769216 | bytes 11534592 | tf_op jit(solution)/shard_map/tke,kb->tbe/dot_general | solution.py:21
  77.3 26.8 %reduce-scatter.2.cloned.1.call-done = f32[8,128,128]{2,1,0:T(8,128)} async-done(((f32[64,128,128]{2,1,0:T(8,128)}), f32[8,128,128]{2,1,0:T(8,128)}) %reduce-scatter.2.cloned.1.call-update) | async-done | bytes 524304 | tf_op jit(solution)/shard_map/reduce_scatter | solution.py:55
  104.1 5.6 %fusion.24 = bf16[64,128,256]{2,1,0:T(8,128)(2,1)} fusion(bf16[64,128,128]{2,1,0:T(8,128)(2,1)S(1)} %copy-done.3, bf16[256,64,128]{0,2,1:T(8,128)(2,1)} %copy.11), kind=kOutput, calls=%fused_computation.26 | convolution fusion | flops 536870912 | bytes 10485760 | tf_op jit(solution)/shard_map/tkf,kfd->tkd/dot_general | solution.py:42
  109.8 4.9 %copy.26 = bf16[32,8,112,128]{3,1,2,0:T(8,128)(2,1)} copy(bf16[32,8,112,128]{3,2,1,0:T(8,128)(2,1)S(1)} %bitcast.47) | data formatting | bytes 14680064
  114.7 6.5 %copy.13 = bf16[64,128,256]{1,0,2:T(8,128)(2,1)} copy(bf16[64,128,256]{2,1,0:T(8,128)(2,1)} %fusion.24) | data formatting | bytes 8388608 | tf_op jit(solution)/shard_map/tkf,kfd->tkd/dot_general | solution.py:42
  121.2 2.9 %fusion.11 = bf16[32,256,128]{2,0,1:T(8,128)(2,1)S(1)} fusion(bf16[64,128,256]{1,0,2:T(8,128)(2,1)} %copy.13, s32[64]{0:T(128)S(1)} %get-tuple-element.4), kind=kOutput, calls=%fused_computation.13 | convolution fusion | flops 134219776 | bytes 6291712 | tf_op jit(solution)/shard_map/tke,kb->tbe/dot_general | solution.py:21
  124.1 21.0 %all-reduce.6.cloned.1.call-done = f32[8,128,128]{2,1,0:T(8,128)} async-done(((f32[8,128,128]{2,1,0:T(8,128)}), f32[8,128,128]{2,1,0:T(8,128)}) %all-reduce.6.cloned.1.call-update) | async-done | bytes 524304 | tf_op jit(solution)/shard_map/psum | solution.py:61
  145.2 1.9 %multiply_reduce_fusion = f32[]{:T(128)} fusion(f32[8,128,128]{2,1,0:T(8,128)} %all-reduce.6.cloned.1.call-done, pred[8]{0:T(512)(128)(4,1)S(1)} %iota_compare_fusion.2), kind=kLoop, calls=%fused_computation.14 | loop fusion | flops 393215 | bytes 524300 | tf_op jit(solution)/shard_map/reduce_sum | solution.py:63
  147.1 2.3 %copy.27 = bf16[32,8,32,128]{3,1,2,0:T(8,128)(2,1)} copy(bf16[32,8,32,128]{3,2,1,0:T(8,128)(2,1)S(1)} %bitcast.48) | data formatting | bytes 4194304
  149.4 13.3 %all-reduce.3 = (f32[]{:T(128)}, f32[]{:T(128)}) all-reduce(f32[]{:T(128)} %multiply_reduce_fusion, f32[]{:T(128)S(6)} %mul.14), channel_id=1, replica_groups=mesh['fsdp'=8,'dp'=4] {'fsdp'}, use_global_device_ids=true, to_apply=%region_3.4 | all-reduce | flops 2 | bytes 16 | tf_op jit(solution)/shard_map/psum | solution.py:65
  164.0 0.9 select_multiply_fusion
  (28 shorter events, 0.6 us)
Async XLA Ops:
  7.2 46.5 %all-gather.2.cloned.1.call-start = ((), (), s32[]{:S(2)}) async-start(), calls=%async_computation.1 | async-start | bytes 2359296 | tf_op jit(solution)/shard_map/all_gather | solution.py:38
  9.6 94.5 %reduce-scatter.2.cloned.1.call-start = ((), (), s32[]{:S(2)}) async-start(), calls=%async_computation.2 | async-start | bytes 4718592 | tf_op jit(solution)/shard_map/reduce_scatter | solution.py:55
  9.7 7.9 %copy-start.8 = (u32[32]{0:T(128)S(1)}, u32[32]{0:T(128)}, u32[]{:S(2)}) copy-start(u32[32]{0:T(128)} %constant.18) | copy-start | bytes 388
  9.7 9.0 %copy-start.6 = (s32[8]{0:T(128)S(1)}, s32[8]{0:T(128)}, u32[]{:S(2)}) copy-start(s32[8]{0:T(128)} %param.10) | copy-start | bytes 100
  9.7 9.3 %copy-start.7 = (s32[8]{0:T(128)S(1)}, s32[8]{0:T(128)}, u32[]{:S(2)}) copy-start(s32[8]{0:T(128)} %param.9) | copy-start | bytes 100
  35.3 7.1 %copy-start.5 = (bf16[256,4096]{1,0:T(8,128)(2,1)S(1)}, bf16[256,4096]{1,0:T(8,128)(2,1)}, u32[]{:S(2)}) copy-start(bf16[256,4096]{1,0:T(8,128)(2,1)} %param.7) | copy-start | bytes 6291460
  42.8 3.3 %copy-start = (bf16[256,64,128]{0,2,1:T(8,128)(2,1)S(1)}, bf16[256,64,128]{0,2,1:T(8,128)(2,1)}, u32[]{:S(2)}) copy-start(bf16[256,64,128]{0,2,1:T(8,128)(2,1)} %copy.11) | copy-start | bytes 12582916
  44.1 2.0 %copy-start.1 = (bf16[256,64,128]{2,1,0:T(8,128)(2,1)}, bf16[256,64,128]{2,1,0:T(8,128)(2,1)S(1)}, u32[]{:S(2)}) copy-start(bf16[256,64,128]{2,1,0:T(8,128)(2,1)S(1)} %convert_bitcast_fusion) | copy-start | bytes 12582916
  53.4 91.8 %all-reduce.6.cloned.1.call-start = ((), (), s32[]{:S(2)}) async-start(), calls=%async_computation.3 | async-start | bytes 1048576 | tf_op jit(solution)/shard_map/psum | solution.py:61
  69.7 34.5 %copy-start.3 = (bf16[64,128,128]{2,1,0:T(8,128)(2,1)S(1)}, bf16[64,128,128]{2,1,0:T(8,128)(2,1)}, u32[]{:S(2)}) copy-start(bf16[64,128,128]{2,1,0:T(8,128)(2,1)} %all-gather.2.cloned.1.call-done) | copy-start | bytes 6291460
  104.1 5.6 %copy-start.2 = (bf16[112,256,128]{2,0,1:T(8,128)(2,1)S(1)}, bf16[112,256,128]{2,0,1:T(8,128)(2,1)}, u32[]{:S(2)}) copy-start(bf16[112,256,128]{2,0,1:T(8,128)(2,1)} %fusion.4) | copy-start | bytes 22020100
  145.2 18.9 %copy-start.4 = (f32[8,128,128]{2,1,0:T(8,128)S(1)}, f32[8,128,128]{2,1,0:T(8,128)}, u32[]{:S(2)}) copy-start(f32[8,128,128]{2,1,0:T(8,128)} %all-reduce.6.cloned.1.call-done) | copy-start | bytes 1572868
Sparse Core Ops, SparseCore 0:
  10.4 30.5 all-gather.1
  53.5 50.5 reduce-scatter.1
  106.4 38.6 all-reduce.5
where the time goes:
time: 172 us; the launch traced here: 171 us
  waiting for transfers between devices  47.9 us (28%)
  matrix products  40.4 us (23%)
  local copies, waits for them, and re-layouts  38.9 us (23%)
  blocking collectives  23 us (13%)
  between operations  16.4 us (10%)
  other arithmetic  4.57 us (3%)
    reduce_scatter x1, waiting for transfers between devices, shards(): lax.psum_scatter(jnp.einsum('tkf,tkd->kfd', picked, upstream, preferred_e...  26.8 us
    psum x1, waiting for transfers between devices, shards(): summed = lax.psum(owned, 'dp')  21 us
    unnamed x27, local copies, waits for them, and re-layouts  18.6 us
    psum x1, blocking collectives, shards(): squares, entries = lax.psum((local_squares, local_entries), 'fsdp')  13.3 us
    dot_general x2, matrix products, place_blocks(): return jnp.einsum('tke,kb->tbe', partial_value, table)  10.5 us
    unnamed x1, blocking collectives  9.69 us
    dot_general x1, matrix products, shards(): jnp.einsum('tkd,kfd->tkf', upstream, gathered, preferred_element_type=jnp...  9.41 us
    dot_general x2, matrix products, select_blocks(): jnp.einsum('tbe,kb->tke', blocks, table, preferred_element_type=jnp.float32)  7.66 us
  transfers between devices with their start and end apart: 3, of which 2 were waited for; matrix products, arithmetic and copies ran while one was open for 44% of the time, Pallas kernels for 0%

commit v1 on v0

v1 whole, which is shorter than its diff:
```python
import functools
import math

import jax
import jax.numpy as jnp
from jax import lax
from jax.experimental import pallas as pl
from jax.experimental.pallas import tpu as pltpu
from jax.sharding import PartitionSpec as P

MESH = pl.DeviceIdType.MESH
F32 = jnp.float32
BF16 = jnp.bfloat16


def exchange_kernel(
    n, dp, root,
    rows_s, cols_s, cnt_s, tiles_hbm, hid_hbm, cot_hbm,
    meta_out, tiles_out, wg_out,
    hid_v, cot_v, tiles_v, meta_v, meta_s, acc, sbuf, rbuf, fin, zs, zr, za, sqz, sqf,
    in_sem, out_sem, meta_ss, meta_rs, ag_ss, ag_rs, rs_ss, rs_rs,
    zs_ss, zs_rs, za_ss, za_rs, qz_ss, qz_rs, qf_ss, qf_rs,
):
    me = lax.axis_index("fsdp")
    z = lax.axis_index("dp")
    maxb, edge = tiles_hbm.shape[0], tiles_hbm.shape[1]
    half = maxb // 2
    per = maxb // dp
    stages = n.bit_length() - 1
    chip_bits = stages - 1
    orders = [list(range(1, stages)), list(range(stages - 1, 0, -1))]
    core = lax.rem(me, 2)

    def bit_of(b):
        return lax.rem(me // (2 ** b), 2)

    def flip(value_me, b):
        return value_me + (1 - 2 * bit_of(b)) * (2 ** b)

    def fetch(source, target, sem):
        def step(i, carry):
            at = pl.ds(pl.multiple_of(i * edge, edge), edge)
            pltpu.make_async_copy(source.at[:, at], target.at[i], sem).start()
            return carry
        lax.fori_loop(0, target.shape[0], step, 0)

    own_copy = pltpu.make_async_copy(tiles_hbm, tiles_v.at[me], in_sem.at[2])
    own_copy.start()
    fetch(cot_hbm, cot_v, in_sem.at[1])
    fetch(hid_hbm, hid_v, in_sem.at[0])

    barrier = pltpu.get_barrier_semaphore()
    for k in range(1, n):
        pl.semaphore_signal(
            barrier, inc=1, device_id={"fsdp": lax.rem(me + k, n)}, device_id_type=MESH
        )
    for k in range(1, dp):
        pl.semaphore_signal(
            barrier, inc=1, device_id={"dp": lax.rem(z + k, dp)}, device_id_type=MESH
        )
    lane = lax.broadcasted_iota(jnp.int32, (8, 128), 1)
    sub = lax.broadcasted_iota(jnp.int32, (8, 128), 0)
    meta = jnp.where(sub == 2, cnt_s[0], 0)
    for j in range(maxb):
        meta = jnp.where((sub == 0) & (lane == j), rows_s[j], meta)
        meta = jnp.where((sub == 1) & (lane == j), cols_s[j], meta)
    meta_v[me] = meta
    own_copy.wait()
    pl.semaphore_wait(barrier, n - 1 + dp - 1)

    meta_copies = []
    for k in range(1, n):
        copy = pltpu.make_async_remote_copy(
            meta_v.at[me], meta_v.at[me], meta_ss.at[k - 1], meta_rs.at[k - 1],
            device_id={"fsdp": lax.rem(me + k, n)}, device_id_type=MESH,
        )
        copy.start()
        meta_copies.append(copy)

    ag_copies = {}

    def ag_send(p, i, e):
        bits = orders[p] + [0]
        owner = me
        for t in range(len(bits)):
            if (e >> t) & 1:
                owner = flip(owner, bits[t])
        piece = tiles_v.at[owner, pl.ds(p * half, half)]
        where = 2 ** i - 1 + e
        copy = pltpu.make_async_remote_copy(
            piece, piece, ag_ss.at[p, where], ag_rs.at[p, where],
            device_id={"fsdp": flip(me, bits[i])}, device_id_type=MESH,
        )
        copy.start()
        ag_copies[p, i, e] = copy

    for i in range(stages):
        for p in range(2):
            ag_send(p, i, 0)

    for copy in meta_copies:
        copy.wait_recv()
    to_smem = pltpu.make_async_copy(meta_v, meta_s, in_sem.at[3])
    to_smem.start()
    to_smem.wait()
    meta_back = pltpu.make_async_copy(meta_v, meta_out, out_sem.at[0])
    meta_back.start()
    pltpu.make_async_copy(cot_v, cot_v, in_sem.at[1]).wait()
    pltpu.make_async_copy(hid_v, hid_v, in_sem.at[0]).wait()

    def owner_at(p, e, core_bit):
        owner = core_bit
        for t, b in enumerate(orders[p]):
            ebit = lax.rem(e // (2 ** (chip_bits - 1 - t)), 2)
            owner = owner + lax.rem(bit_of(b) + 1 + ebit, 2) * (2 ** b)
        return owner

    def term(owner, j):
        return lax.dot_general(
            hid_v[meta_s[owner, 0, j]], cot_v[meta_s[owner, 1, j]],
            (((0,), (0,)), ((), ())), preferred_element_type=F32,
        )

    chips = n // 2
    offsets = [0]
    for t in range(stages):
        offsets.append(offsets[-1] + (n >> (t + 1)))

    def rs_copy(p, t, e):
        where = offsets[t] + e
        bit = 0 if t == 0 else orders[p][t - 1]
        return pltpu.make_async_remote_copy(
            sbuf.at[p, where], rbuf.at[p, where], rs_ss.at[p, where], rs_rs.at[p, where],
            device_id={"fsdp": flip(me, bit)}, device_id_type=MESH,
        )

    def foreign(e, carry):
        for p in range(2):
            owner = owner_at(p, e, 1 - core)
            for j in range(half):
                sbuf[p, e, j] = term(owner, p * half + j).astype(BF16)
            rs_copy(p, 0, e).start()
        return carry

    lax.fori_loop(0, chips, foreign, 0)

    for i in range(chip_bits):
        for p in range(2):
            for e in range(2 ** i):
                ag_copies[p, i, e].wait_recv()
                for i2 in range(i + 1, stages):
                    ag_send(p, i2, e + 2 ** i)

    def own(e, carry):
        for p in range(2):
            owner = owner_at(p, e, core)
            for j in range(half):
                acc[p, e, j] = term(owner, p * half + j)
        return carry

    lax.fori_loop(0, chips, own, 0)

    start = 0
    for t in range(stages):
        m = n >> (t + 1)
        sent = m // 2
        for e in range(m):
            for p in range(2):
                rs_copy(p, t, e).wait_recv()
                total = acc[p, start + e] + rbuf[p, offsets[t] + e].astype(F32)
                if e < sent:
                    sbuf[p, offsets[t + 1] + e] = total.astype(BF16)
                    rs_copy(p, t + 1, e).start()
                elif m > 1:
                    acc[p, start + e] = total
                else:
                    fin[pl.ds(p * half, half)] = total
                    for q in range(half // per):
                        zs[p * (half // per) + q] = total[q * per:(q + 1) * per].astype(BF16)
        start += sent

    def z_peer(r):
        return lax.rem(z + r, dp)

    z_copies = []
    for r in range(1, dp):
        copy = pltpu.make_async_remote_copy(
            zs.at[z_peer(r)], zr.at[r - 1], zs_ss.at[r - 1], zs_rs.at[r - 1],
            device_id={"dp": z_peer(r)}, device_id_type=MESH,
        )
        copy.start()
        z_copies.append(copy)

    for p in range(2):
        for e in range(2 ** chip_bits):
            ag_copies[p, chip_bits, e].wait_recv()
    tiles_back = pltpu.make_async_copy(tiles_v, tiles_out, out_sem.at[1])
    tiles_back.start()

    piece = fin[pl.ds(z * per, per)]
    for r in range(1, dp):
        z_copies[r - 1].wait_recv()
        piece = piece + zr[r - 1].astype(F32)
    slot = z * per + lax.broadcasted_iota(jnp.int32, piece.shape, 0)
    piece = piece * jnp.clip(cnt_s[0] - slot, 0, 1).astype(F32)
    za[z] = piece.astype(BF16)
    sqz[z] = jnp.sum((piece * piece).reshape(-1, 8, 128), axis=0)
    a_copies, q_copies = [], []
    for r in range(1, dp):
        copy = pltpu.make_async_remote_copy(
            sqz.at[z], sqz.at[z], qz_ss.at[r - 1], qz_rs.at[r - 1],
            device_id={"dp": z_peer(r)}, device_id_type=MESH,
        )
        copy.start()
        q_copies.append(copy)
    for r in range(1, dp):
        copy = pltpu.make_async_remote_copy(
            za.at[z], za.at[z], za_ss.at[r - 1], za_rs.at[r - 1],
            device_id={"dp": z_peer(r)}, device_id_type=MESH,
        )
        copy.start()
        a_copies.append(copy)
    for copy in q_copies:
        copy.wait_recv()
    sqf[me] = jnp.sum(sqz[...], axis=0)
    f_copies = []
    for k in range(1, n):
        copy = pltpu.make_async_remote_copy(
            sqf.at[me], sqf.at[me], qf_ss.at[k - 1], qf_rs.at[k - 1],
            device_id={"fsdp": lax.rem(me + k, n)}, device_id_type=MESH,
        )
        copy.start()
        f_copies.append(copy)
    entries = meta_s[0, 2, 0]
    for k in range(1, n):
        entries = entries + meta_s[k, 2, 0]
    for copy in a_copies + f_copies:
        copy.wait_recv()
    squares = jnp.sum(jnp.sum(sqf[...], axis=0), axis=(0, 1), keepdims=True)
    live = jnp.full((1, 1), entries, jnp.int32).astype(F32) * edge * edge
    spread = jnp.sqrt(squares / live)
    factor = jnp.minimum(1.0, 0.5 * root / spread) / root
    for q in range(dp):
        for i in range(per):
            wg_out[q * per + i] = za[q, i].astype(F32) * factor

    for copy in meta_copies + list(ag_copies.values()) + z_copies + q_copies + a_copies + f_copies:
        copy.wait_send()
    for t in range(stages):
        for e in range(n >> (t + 1)):
            for p in range(2):
                rs_copy(p, t, e).wait_send()
    meta_back.wait()
    tiles_back.wait()


def project_kernel(
    n, maxb,
    meta_s, tiles_hbm, hid_hbm, cot_hbm,
    layer_hbm, grad_hbm,
    tiles_v, cot_v, hid_v, gacc, gout, lacc, lout, zero_v,
    row_left, row_seen, col_left, col_seen,
    in_sem, hid_sem, g_sem, l_sem,
):
    edge = zero_v.shape[1]
    tile_copy = pltpu.make_async_copy(tiles_hbm, tiles_v, in_sem.at[0])
    cot_copy = pltpu.make_async_copy(cot_hbm, cot_v, in_sem.at[1])
    tile_copy.start()
    cot_copy.start()
    zero_v[...] = jnp.zeros_like(zero_v)

    def clear(left, seen):
        def step(i, carry):
            left[i] = 0
            seen[i] = 0
            return carry
        lax.fori_loop(0, left.shape[0], step, 0)

    clear(row_left, row_seen)
    clear(col_left, col_seen)

    def columns(i):
        return pl.ds(pl.multiple_of(i * edge, edge), edge)

    def each_live(visit):
        def owner(o, carry):
            def slot(j, inner):
                visit(o, j, meta_s[o, 0, j], meta_s[o, 1, j])
                return inner
            return lax.fori_loop(0, meta_s[o, 2, 0], slot, carry)
        lax.fori_loop(0, n, owner, 0)

    def fetch(o, j, row, col):
        pltpu.make_async_copy(hid_hbm.at[:, columns(row)], hid_v.at[o, j], hid_sem).start()
        row_left[row] = row_left[row] + 1
        col_left[col] = col_left[col] + 1

    each_live(fetch)

    def blank(left, target, sem):
        def step(i, carry):
            @pl.when(left[i] == 0)
            def _():
                pltpu.make_async_copy(zero_v, target.at[:, columns(i)], sem).start()
            return carry
        lax.fori_loop(0, left.shape[0], step, 0)

    blank(row_left, grad_hbm, g_sem)
    blank(col_left, layer_hbm, l_sem)
    tile_copy.wait()
    cot_copy.wait()

    def add_block(at, value, left, seen, total, out, target, sem):
        remaining = left[at] - 1
        first = seen[at] == 0
        left[at] = remaining
        seen[at] = 1

        @pl.when(first & (remaining == 0))
        def _():
            out[at] = value.astype(BF16)

        @pl.when(first & (remaining > 0))
        def _():
            total[at] = value

        @pl.when(jnp.logical_not(first) & (remaining > 0))
        def _():
            total[at] = total[at] + value

        @pl.when(jnp.logical_not(first) & (remaining == 0))
        def _():
            out[at] = (total[at] + value).astype(BF16)

        @pl.when(remaining == 0)
        def _():
            pltpu.make_async_copy(out.at[at], target.at[:, columns(at)], sem).start()

    def backward(o, j, row, col):
        value = lax.dot_general(
            cot_v[:, columns(col)], tiles_v[o, j], (((1,), (1,)), ((), ())),
            preferred_element_type=F32,
        )
        add_block(row, value, row_left, row_seen, gacc, gout, grad_hbm, g_sem)

    each_live(backward)

    def arrived(o, j, row, col):
        pltpu.make_async_copy(hid_hbm.at[:, columns(row)], hid_v.at[o, j], hid_sem).wait()

    each_live(arrived)

    def forward(o, j, row, col):
        value = jnp.dot(hid_v[o, j], tiles_v[o, j], preferred_element_type=F32)
        add_block(col, value, col_left, col_seen, lacc, lout, layer_hbm, l_sem)

    each_live(forward)
    pltpu.make_async_copy(grad_hbm, grad_hbm, g_sem).wait()
    pltpu.make_async_copy(layer_hbm, layer_hbm, l_sem).wait()


def shards(n, dp, hidden, cotangent, tiles, tile_rows, tile_cols, counts):
    tokens, width_ff = hidden.shape
    width_model = cotangent.shape[1]
    maxb, edge, _ = tiles.shape
    blocks_ff, blocks_model = width_ff // edge, width_model // edge
    root = math.sqrt(tokens * n * dp)
    half, per = maxb // 2, maxb // dp
    hbm = pl.BlockSpec(memory_space=pl.ANY)
    smem = pl.BlockSpec(memory_space=pltpu.SMEM)
    vmem = pl.BlockSpec(memory_space=pltpu.VMEM)
    dma = pltpu.SemaphoreType.DMA
    meta, gathered, weight_grad = pl.pallas_call(
        functools.partial(exchange_kernel, n, dp, root),
        out_shape=(
            jax.ShapeDtypeStruct((n, 8, 128), jnp.int32),
            jax.ShapeDtypeStruct((n, maxb, edge, edge), BF16),
            jax.ShapeDtypeStruct((maxb, edge, edge), F32),
        ),
        in_specs=[smem, smem, smem, hbm, hbm, hbm],
        out_specs=(hbm, hbm, vmem),
        scratch_shapes=[
            pltpu.VMEM((blocks_ff, tokens, edge), BF16),
            pltpu.VMEM((blocks_model, tokens, edge), BF16),
            pltpu.VMEM((n, maxb, edge, edge), BF16),
            pltpu.VMEM((n, 8, 128), jnp.int32),
            pltpu.SMEM((n, 8, 128), jnp.int32),
            pltpu.VMEM((2, n // 2, half, edge, edge), F32),
            pltpu.VMEM((2, n - 1, half, edge, edge), BF16),
            pltpu.VMEM((2, n - 1, half, edge, edge), BF16),
            pltpu.VMEM((maxb, edge, edge), F32),
            pltpu.VMEM((dp, per, edge, edge), BF16),
            pltpu.VMEM((dp - 1, per, edge, edge), BF16),
            pltpu.VMEM((dp, per, edge, edge), BF16),
            pltpu.VMEM((dp, 8, 128), F32),
            pltpu.VMEM((n, 8, 128), F32),
            dma((4,)), dma((2,)),
            dma((n - 1,)), dma((n - 1,)),
            dma((2, n - 1)), dma((2, n - 1)),
            dma((2, n - 1)), dma((2, n - 1)),
            dma((dp - 1,)), dma((dp - 1,)),
            dma((dp - 1,)), dma((dp - 1,)),
            dma((dp - 1,)), dma((dp - 1,)),
            dma((n - 1,)), dma((n - 1,)),
        ],
        compiler_params=pltpu.CompilerParams(
            collective_id=0, has_side_effects=True, vmem_limit_bytes=60 * 2 ** 20
        ),
        name="exchange",
    )(tile_rows, tile_cols, counts, tiles, hidden, cotangent)

    layer_out, hidden_grad = pl.pallas_call(
        functools.partial(project_kernel, n, maxb),
        out_shape=(
            jax.ShapeDtypeStruct(cotangent.shape, BF16),
            jax.ShapeDtypeStruct(hidden.shape, BF16),
        ),
        in_specs=[smem, hbm, hbm, hbm],
        out_specs=(hbm, hbm),
        scratch_shapes=[
            pltpu.VMEM((n, maxb, edge, edge), BF16),
            pltpu.VMEM(cotangent.shape, BF16),
            pltpu.VMEM((n, maxb, tokens, edge), BF16),
            pltpu.VMEM((blocks_ff, tokens, edge), F32),
            pltpu.VMEM((blocks_ff, tokens, edge), BF16),
            pltpu.VMEM((blocks_model, tokens, edge), F32),
            pltpu.VMEM((blocks_model, tokens, edge), BF16),
            pltpu.VMEM((tokens, edge), BF16),
            pltpu.SMEM((blocks_ff,), jnp.int32),
            pltpu.SMEM((blocks_ff,), jnp.int32),
            pltpu.SMEM((blocks_model,), jnp.int32),
            pltpu.SMEM((blocks_model,), jnp.int32),
            dma((2,)), dma, dma, dma,
        ],
        compiler_params=pltpu.CompilerParams(vmem_limit_bytes=62 * 2 ** 20),
        name="project",
    )(meta, gathered, hidden, cotangent)
    return layer_out, hidden_grad, weight_grad


def solution(mesh):
    placed = (
        P(("fsdp", "dp"), None),
        P(("fsdp", "dp"), None),
        P("fsdp", None, None),
        P("fsdp"),
        P("fsdp"),
        P("fsdp"),
    )
    return jax.shard_map(
        functools.partial(shards, mesh.shape["fsdp"], mesh.shape["dp"]),
        mesh=mesh,
        in_specs=placed,
        out_specs=(P(("fsdp", "dp"), None), P(("fsdp", "dp"), None), P("fsdp", None, None)),
        check_vma=False,
    )
```

time: 172 us -> 66 us (0.38)
  Pallas kernels: 0 us -> 62.9 us
  waiting for transfers between devices: 47.9 us -> 0 us
  matrix products: 40.4 us -> 0 us
  local copies, waits for them, and re-layouts: 38.9 us -> 0.8 us
  blocking collectives: 23 us -> 0 us
  between operations: 16.4 us -> 1.31 us
  other arithmetic: 4.57 us -> 0 us
    pallas_call x0 -> x2, Pallas kernels: none -> 62.9 us  [the longest x1 46.2 us: shards(): pl.pallas_call(functools.partial(exchange_kernel, n, dp, root), out_shape...]
    dot_general x7 -> x0, matrix products: 40.4 us -> none  [the longest x2 10.5 us: place_blocks(): return jnp.einsum('tke,kb->tbe', partial_value, table)]
    reduce_scatter x1 -> x0, waiting for transfers between devices: 26.8 us -> none  [shards(): lax.psum_scatter(jnp.einsum('tkf,tkd->kfd', picked, upstream, preferred_e...]
    psum x1 -> x0, waiting for transfers between devices: 21 us -> none  [shards(): summed = lax.psum(owned, 'dp')]
    unnamed x27 -> x3, local copies, waits for them, and re-layouts: 18.6 us -> 0.8 us
    psum x1 -> x0, blocking collectives: 13.3 us -> none  [shards(): squares, entries = lax.psum((local_squares, local_entries), 'fsdp')]
    dot_general x2 -> x0, local copies, waits for them, and re-layouts: 13.2 us -> none  [the longest x1 6.63 us: shards(): jnp.einsum('tkd,kfd->tkf', upstream, gathered, preferred_element_type=jnp...]
    unnamed x1 -> x0, blocking collectives: 9.69 us -> none
  transfers between devices with their start and end apart: 3 -> 0, of which waited for: 2 -> 0; matrix products, arithmetic and copies ran while one was open for 44% -> 0% of each run, Pallas kernels for 0% -> 0%
where the time goes in v1:
time: 66 us; the launch traced here: 65 us
  Pallas kernels  62.9 us (95%)
  between operations  1.31 us (2%)
  local copies, waits for them, and re-layouts  0.8 us (1%)
    pallas_call x1, Pallas kernels, shards(): pl.pallas_call(functools.partial(exchange_kernel, n, dp, root), out_shape...  46.2 us
    pallas_call x1, Pallas kernels, shards(): pl.pallas_call(functools.partial(project_kernel, n, maxb), out_shape=(jax...  16.7 us

profile of v1, /device:TPU:0, one launch (start us, length us, event | category | flops | bytes accessed | tf_op | source)
XLA Modules:
  0.0 65.0 jit_solution(1219945699582174318)
XLA Ops:
  1.3 46.2 %exchange.1 = (s32[8,8,128]{2,1,0:T(8,128)}, bf16[8,8,128,128]{3,2,1,0:T(8,128)(2,1)}, f32[8,128,128]{2,1,0:T(8,128)}) custom-call(s32[8]{0:T(128)} %rows_s.1, s32[8]{0:T(128)} %cols_s.1, s32[1]{0:T(128)S(6)} %copy.10.cnt_s, bf16[8,128,128]{2,1,0:T(8,128)(2,1)} %tiles_hbm.1, bf16[256,14336]{1,0:T(8,128)(2,1)} %hid_hbm.3, bf16[256,4096]{1,0:T(8,128)(2,1)} %cot_hbm.3), custom_call_target="tpu_custom_call" | custom-call | tf_op jit(solution)/shard_map/exchange/pallas_call | solution.py:373
  47.5 0.0 copy-start
  47.5 16.7 %project.1 = (bf16[256,4096]{1,0:T(8,128)(2,1)}, bf16[256,14336]{1,0:T(8,128)(2,1)}) custom-call(s32[8,8,128]{2,1,0:T(8,128)} %get-tuple-element.8.meta_s, bf16[8,8,128,128]{3,2,1,0:T(8,128)(2,1)} %get-tuple-element.9.tiles_hbm, bf16[256,14336]{1,0:T(8,128)(2,1)} %hid_hbm.3, bf16[256,4096]{1,0:T(8,128)(2,1)} %cot_hbm.3), custom_call_target="tpu_custom_call" | custom-call | tf_op jit(solution)/shard_map/project/pallas_call | solution.py:412
  64.2 0.0 copy-done
  64.2 0.8 %copy.11 = f32[8,128,128]{2,1,0:T(8,128)} copy(f32[8,128,128]{2,1,0:T(8,128)S(1)} %copy-done) | data formatting | bytes 1048576
Async XLA Ops:
  47.5 16.7 %copy-start = (f32[8,128,128]{2,1,0:T(8,128)S(1)}, f32[8,128,128]{2,1,0:T(8,128)}, u32[]{:S(2)}) copy-start(f32[8,128,128]{2,1,0:T(8,128)} %get-tuple-element.18) | copy-start | bytes 1572868

commit v2 on v1

--- a/solution.py
+++ b/solution.py
@@ -258,7 +258,7 @@
     n, maxb,
     meta_s, tiles_hbm, hid_hbm, cot_hbm,
     layer_hbm, grad_hbm,
-    tiles_v, cot_v, hid_v, gacc, gout, lacc, lout, zero_v,
+    tiles_v, cot_v, hid_v, gacc, gout, lacc, lout, zero_v, values,
     row_left, row_seen, col_left, col_seen,
     in_sem, hid_sem, g_sem, l_sem,
 ):
@@ -318,43 +318,57 @@
 
         @pl.when(first & (remaining == 0))
         def _():
-            out[at] = value.astype(BF16)
+            out[at] = value[...].astype(BF16)
 
         @pl.when(first & (remaining > 0))
         def _():
-            total[at] = value
-
-        @pl.when(jnp.logical_not(first) & (remaining > 0))
+            total[at] = value[...]
+
+        @pl.when(jnp.logical_not(first))
         def _():
-            total[at] = total[at] + value
-
-        @pl.when(jnp.logical_not(first) & (remaining == 0))
-        def _():
-            out[at] = (total[at] + value).astype(BF16)
+            summed = total[at] + value[...]
+            total[at] = summed
+            out[at] = summed.astype(BF16)
 
         @pl.when(remaining == 0)
         def _():
             pltpu.make_async_copy(out.at[at], target.at[:, columns(at)], sem).start()
 
-    def backward(o, j, row, col):
-        value = lax.dot_general(
-            cot_v[:, columns(col)], tiles_v[o, j], (((1,), (1,)), ((), ())),
-            preferred_element_type=F32,
-        )
-        add_block(row, value, row_left, row_seen, gacc, gout, grad_hbm, g_sem)
-
-    each_live(backward)
+    def backward(o, carry):
+        for j in range(maxb):
+            values[j] = lax.dot_general(
+                cot_v[:, columns(meta_s[o, 1, j])], tiles_v[o, j], (((1,), (1,)), ((), ())),
+                preferred_element_type=F32,
+            )
+
+        def slot(j, inner):
+            add_block(
+                meta_s[o, 0, j], values.at[j], row_left, row_seen, gacc, gout, grad_hbm, g_sem
+            )
+            return inner
+
+        return lax.fori_loop(0, meta_s[o, 2, 0], slot, carry)
+
+    lax.fori_loop(0, n, backward, 0)
 
     def arrived(o, j, row, col):
         pltpu.make_async_copy(hid_hbm.at[:, columns(row)], hid_v.at[o, j], hid_sem).wait()
 
     each_live(arrived)
 
-    def forward(o, j, row, col):
-        value = jnp.dot(hid_v[o, j], tiles_v[o, j], preferred_element_type=F32)
-        add_block(col, value, col_left, col_seen, lacc, lout, layer_hbm, l_sem)
-
-    each_live(forward)
+    def forward(o, carry):
+        for j in range(maxb):
+            values[j] = jnp.dot(hid_v[o, j], tiles_v[o, j], preferred_element_type=F32)
+
+        def slot(j, inner):
+            add_block(
+                meta_s[o, 1, j], values.at[j], col_left, col_seen, lacc, lout, layer_hbm, l_sem
+            )
+            return inner
+
+        return lax.fori_loop(0, meta_s[o, 2, 0], slot, carry)
+
+    lax.fori_loop(0, n, forward, 0)
     pltpu.make_async_copy(grad_hbm, grad_hbm, g_sem).wait()
     pltpu.make_async_copy(layer_hbm, layer_hbm, l_sem).wait()
 
@@ -426,6 +440,7 @@
             pltpu.VMEM((blocks_model, tokens, edge), F32),
             pltpu.VMEM((blocks_model, tokens, edge), BF16),
             pltpu.VMEM((tokens, edge), BF16),
+            pltpu.VMEM((maxb, tokens, edge), F32),
             pltpu.SMEM((blocks_ff,), jnp.int32),
             pltpu.SMEM((blocks_ff,), jnp.int32),
             pltpu.SMEM((blocks_model,), jnp.int32),

time: 66 us -> 61.2 us (0.927); the launches traced: 65 us -> 61.2 us
  Pallas kernels: 62.9 us -> 59.1 us
    pallas_call x1, Pallas kernels: 16.7 us -> 12.8 us  [shards(): pl.pallas_call(functools.partial(project_kernel, n, maxb), out_shape=(jax...]
where the time goes in v2:
time: 61.2 us
  Pallas kernels  59.1 us (97%)
  between operations  1.31 us (2%)
  local copies, waits for them, and re-layouts  0.8 us (1%)
    pallas_call x1, Pallas kernels, shards(): pl.pallas_call(functools.partial(exchange_kernel, n, dp, root), out_shape...  46.2 us
    pallas_call x1, Pallas kernels, shards(): pl.pallas_call(functools.partial(project_kernel, n, maxb), out_shape=(jax...  12.8 us

profile of v2, /device:TPU:0, one launch (start us, length us, event | category | flops | bytes accessed | tf_op | source)
XLA Modules:
  0.0 61.2 jit_solution(6509944032430782735)
XLA Ops:
  1.3 46.2 %exchange.1 = (s32[8,8,128]{2,1,0:T(8,128)}, bf16[8,8,128,128]{3,2,1,0:T(8,128)(2,1)}, f32[8,128,128]{2,1,0:T(8,128)}) custom-call(s32[8]{0:T(128)} %rows_s.1, s32[8]{0:T(128)} %cols_s.1, s32[1]{0:T(128)S(6)} %copy.10.cnt_s, bf16[8,128,128]{2,1,0:T(8,128)(2,1)} %tiles_hbm.1, bf16[256,14336]{1,0:T(8,128)(2,1)} %hid_hbm.3, bf16[256,4096]{1,0:T(8,128)(2,1)} %cot_hbm.3), custom_call_target="tpu_custom_call" | custom-call | tf_op jit(solution)/shard_map/exchange/pallas_call | solution.py:387
  47.5 0.0 copy-start
  47.5 12.8 %project.1 = (bf16[256,4096]{1,0:T(8,128)(2,1)}, bf16[256,14336]{1,0:T(8,128)(2,1)}) custom-call(s32[8,8,128]{2,1,0:T(8,128)} %get-tuple-element.8.meta_s, bf16[8,8,128,128]{3,2,1,0:T(8,128)(2,1)} %get-tuple-element.9.tiles_hbm, bf16[256,14336]{1,0:T(8,128)(2,1)} %hid_hbm.3, bf16[256,4096]{1,0:T(8,128)(2,1)} %cot_hbm.3), custom_call_target="tpu_custom_call" | custom-call | tf_op jit(solution)/shard_map/project/pallas_call | solution.py:426
  60.4 0.0 copy-done
  60.4 0.8 %copy.11 = f32[8,128,128]{2,1,0:T(8,128)} copy(f32[8,128,128]{2,1,0:T(8,128)S(1)} %copy-done) | data formatting | bytes 1048576
Async XLA Ops:
  47.5 12.9 %copy-start = (f32[8,128,128]{2,1,0:T(8,128)S(1)}, f32[8,128,128]{2,1,0:T(8,128)}, u32[]{:S(2)}) copy-start(f32[8,128,128]{2,1,0:T(8,128)} %get-tuple-element.18) | copy-start | bytes 1572868
